TPU v7x, 32 devices: a whole 2x2x4 slice. The times are simulated.
32 devices in a mesh: dp: 8 (over y, x, core), fsdp: 4 (over z).
Axes of the slice: x: 2, y: 2, z: 4, core: 2. Of those that a mesh axis runs over, the one named last changes fastest.
Arguments:
- acts: bfloat16 [16384, 8192], P(('dp', 'fsdp')), may hold values from -6 to 6
- grad_out: bfloat16 [16384, 1024], P(('dp', 'fsdp')), may hold values from -6 to 6
- codes: int32 [128, 16, 1024], P('fsdp'), may hold values from 0 to 65535
- scale_codes: int32 [128, 1024], P('fsdp'), may hold values from 0 to 255
- col_scale: float32 [1024], replicated, may hold values from 0.03 to 0.3
- down_adapter: bfloat16 [64, 8192], P(None, 'fsdp'), may hold values from -0.1796875 to 0.1796875
- up_adapter: bfloat16 [64, 1024], P(None, 'fsdp'), may hold values from -0.1875 to 0.1875
Outputs:
- input_gradient: bfloat16 [16384, 8192], P(('dp', 'fsdp'))
- grad_down: float32 [64, 8192], P(None, 'fsdp')
- grad_up: float32 [64, 1024], P(None, 'fsdp')
All inputs are finite; a program needn't handle non-finite values.
Results may differ from a plain program's by a relative error of at most 0.0059.
Values may be sent and summed in bfloat16 or wider, within the bound.
A program may use at most 128 MiB of HBM per device.

v0:
```python
import jax
import jax.numpy as jnp
from jax import lax
from jax.sharding import PartitionSpec as P

adapter_scale = 0.5
nf4_table = [
    -1.0,
    -0.6961928009986877,
    -0.5250730514526367,
    -0.39491748809814453,
    -0.28444138169288635,
    -0.18477343022823334,
    -0.09105003625154495,
    0.0,
    0.07958029955625534,
    0.16093020141124725,
    0.24611230194568634,
    0.33791524171829224,
    0.44070982933044434,
    0.5626170039176941,
    0.7229568362236023,
    1.0,
]


def dequantize(codes, scale_codes, col_scale):
    block_count = codes.shape[0]
    columns = codes.shape[2]
    nibbles = jnp.stack([codes >> 4 * nibble_pos & 15 for nibble_pos in range(4)], axis=2)
    levels = jnp.zeros(nibbles.shape, jnp.float32)
    for position, quantum in enumerate(nf4_table):
        levels = jnp.where(nibbles == position, jnp.float32(quantum), levels)
    absmax = (scale_codes.astype(jnp.float32) + 1.0) / 256.0 * col_scale[None, :]
    weight = levels * absmax[:, None, None, :]
    return weight.reshape(block_count * 64, columns).astype(jnp.bfloat16)


def local(acts, grad_out, codes, scale_codes, col_scale, down_adapter, up_adapter):
    down_full, up_full = (
        lax.all_gather(down_adapter, "fsdp", axis=1, tiled=True),
        lax.all_gather(up_adapter, "fsdp", axis=1, tiled=True),
    )
    mixed = jnp.dot(grad_out, up_full.T, preferred_element_type=jnp.float32).astype(jnp.bfloat16)
    lowered = jnp.dot(acts, down_full.T, preferred_element_type=jnp.float32).astype(jnp.bfloat16)
    token_count = acts.shape[0] * lax.axis_size("dp") * lax.axis_size("fsdp")
    scale_factor = adapter_scale * float(token_count) ** (-0.5)
    local_rows = dequantize(codes, scale_codes, col_scale)
    frozen_base = lax.dot_general(
        grad_out,
        lax.all_gather(local_rows, "fsdp", axis=0, tiled=True),
        (((1,), (1,)), ((), ())),
        preferred_element_type=jnp.float32,
    )
    operand_side = jnp.dot(mixed, down_full, preferred_element_type=jnp.float32)
    input_gradient = (frozen_base + adapter_scale * operand_side).astype(jnp.bfloat16)
    term_down = lax.dot_general(
        mixed, acts, (((0,), (0,)), ((), ())), preferred_element_type=jnp.float32
    )
    term_up = lax.dot_general(
        lowered, grad_out, (((0,), (0,)), ((), ())), preferred_element_type=jnp.float32
    )
    shard_down = lax.psum_scatter(term_down, "fsdp", scatter_dimension=1, tiled=True)
    shard_up = lax.psum_scatter(term_up, "fsdp", scatter_dimension=1, tiled=True)
    summed_down, summed_up = lax.psum((shard_down, shard_up), "dp")
    grad_down = scale_factor * summed_down
    grad_up = scale_factor * summed_up
    return (input_gradient, grad_down, grad_up)


def solution(mesh):
    placed = (
        P(("dp", "fsdp"), None),
        P(("dp", "fsdp"), None),
        P("fsdp", None, None),
        P("fsdp", None),
        P(),
        P(None, "fsdp"),
        P(None, "fsdp"),
    )
    return jax.shard_map(
        local,
        mesh=mesh,
        in_specs=placed,
        out_specs=(P(("dp", "fsdp"), None), P(None, "fsdp"), P(None, "fsdp")),
        check_vma=False,
    )
```

profile of v0, /device:TPU:0, one launch (start us, length us, event | category | flops | bytes accessed | tf_op | source)
XLA Modules:
  0.0 506.7 jit_solution(733886162485765872)
XLA Ops:
  7.2 0.7 all-gather.5.cloned.1.call-update
  8.0 15.3 %all_gather.10 = bf16[64,1024]{1,0:T(8,128)(2,1)S(1)} all-gather(bf16[64,256]{1,0:T(8,128)(2,1)} %param.13), channel_id=1, replica_groups=mesh['dp'=8,'fsdp'=4] {'fsdp'}, dimensions={1}, use_global_device_ids=true | all-gather | bytes 163840 | tf_op jit(solution)/shard_map/all_gather | solution.py:42
  23.7 16.7 %all-gather.5.cloned.1.call-done = bf16[64,8192]{1,0:T(8,128)(2,1)} async-done(((bf16[64,2048]{1,0:T(8,128)(2,1)}), bf16[64,8192]{1,0:T(8,128)(2,1)}) %all-gather.5.cloned.1.call-update) | async-done | bytes 1048592 | tf_op jit(solution)/shard_map/all_gather | solution.py:41
  40.4 7.1 %fusion.2 = f32[64,1024]{1,0:T(8,128)} fusion(bf16[512,1024]{1,0:T(8,128)(2,1)S(1)} %copy-done, bf16[512,8192]{1,0:T(8,128)(2,1)} %param.7, bf16[64,8192]{1,0:T(8,128)(2,1)} %all-gather.5.cloned.1.call-done), kind=kOutput, calls=%fused_computation.11 | convolution fusion | flops 604012544 | bytes 10747904 | tf_op jit(solution)/shard_map/dot_general | solution.py:60
  47.6 6.3 %fusion.4 = f32[64,8192]{1,0:T(8,128)} fusion(bf16[512,64]{0,1:T(8,128)(2,1)S(1)} %convolution_convert_fusion.1, bf16[512,8192]{1,0:T(8,128)(2,1)} %param.7), kind=kOutput, calls=%fused_computation.18 | convolution fusion | flops 536870912 | bytes 10551296 | tf_op jit(solution)/shard_map/dot_general | solution.py:57
  54.1 2.5 and_bitcast_fusion.3
  56.7 1.3 copy-done.1
  58.6 0.7 copy-done.3
  59.3 9.5 %select_select_fusion = f32[32,16,4,1024]{3,1,0,2:T(8,128)} fusion(s32[32,16,1,1024]{3,1,0,2:T(8,128)S(1)} %get-tuple-element.13, s32[32,16,1,1024]{3,1,0,2:T(8,128)S(1)} %get-tuple-element.14, s32[32,16,1,1024]{3,1,0,2:T(8,128)S(1)} %get-tuple-element.12, s32[32,16,1,1024]{3,1,0,2:T(8,128)S(1)} %get-tuple-element.11), kind=kLoop, calls=%fused_computation.3 | loop fusion | flops 69206016 | bytes 16777216 | tf_op jit(solution)/shard_map/jit(_where)/select_n | solution.py:33
  68.8 13.8 %copy.13 = f32[32,16,4,1024]{3,2,1,0:T(4,128)} copy(f32[32,16,4,1024]{3,1,0,2:T(8,128)} %select_select_fusion) | data formatting | bytes 16777216 | tf_op jit(solution)/shard_map/jit(_where)/select_n | solution.py:33
  82.6 10.1 %reshape.73 = f32[2048,1024]{1,0:T(8,128)} reshape(f32[32,16,4,1024]{3,2,1,0:T(4,128)} %copy.13) | data formatting | bytes 16777216 | tf_op jit(solution)/shard_map/jit(_where)/select_n | solution.py:33
  92.7 3.8 fusion.1
  96.5 4.3 copy.12
  100.8 3.6 eq.156
  104.5 5.5 %mul.45 = f32[32,16,4,1024]{3,2,1,0:T(4,128)} broadcast(f32[32,1024]{1,0:T(8,128)S(1)} %add_multiply_fusion), dimensions={0,3} | broadcast | bytes 8519680 | tf_op jit(solution)/shard_map/mul | solution.py:35
  110.0 10.1 %mul.46 = f32[2048,1024]{1,0:T(8,128)} reshape(f32[32,16,4,1024]{3,2,1,0:T(4,128)} %mul.45) | data formatting | bytes 16777216 | tf_op jit(solution)/shard_map/mul | solution.py:35
  120.2 10.4 %multiply_convert_fusion = bf16[2048,1024]{1,0:T(8,128)(2,1)} fusion(f32[2048,1024]{1,0:T(8,128)} %mul.46, pred[2048,1024]{1,0:T(8,128)(4,1)S(1)} %copy-done.4, f32[2048,1024]{1,0:T(8,128)} %reshape.73), kind=kLoop, calls=%fused_computation.4 | loop fusion | flops 6291456 | bytes 23068672 | tf_op jit(solution)/shard_map/convert_element_type | solution.py:36
  130.7 44.5 %all-reduce.3.cloned.1.call-done = (f32[64,2048]{1,0:T(8,128)}, f32[64,256]{1,0:T(8,128)}) async-done(((f32[64,2048]{1,0:T(8,128)}, f32[64,256]{1,0:T(8,128)}), (f32[64,2048]{1,0:T(8,128)}, f32[64,256]{1,0:T(8,128)})) %all-reduce.3.cloned.1.call-update) | async-done | bytes 589840 | tf_op jit(solution)/shard_map/psum | solution.py:65
  175.1 1.5 broadcast_multiply_fusion.1
  176.6 1.9 broadcast_multiply_fusion
  178.5 284.8 %all-gather.3.cloned.1.call-done = bf16[8192,1024]{1,0:T(8,128)(2,1)} async-done(((bf16[2048,1024]{1,0:T(8,128)(2,1)}), bf16[8192,1024]{1,0:T(8,128)(2,1)}) %all-gather.3.cloned.1.call-update) | async-done | bytes 16777232 | tf_op jit(solution)/shard_map/all_gather | solution.py:51
  463.3 15.8 %fusion.3 = f32[8192,512]{1,0:T(8,128)} fusion(bf16[8192,1024]{1,0:T(8,128)(2,1)} %all-gather.3.cloned.1.call-done, bf16[512,1024]{1,0:T(8,128)(2,1)S(1)} %copy-done), kind=kOutput, calls=%fused_computation.17 | convolution fusion | flops 8589934592 | bytes 34603008 | tf_op jit(solution)/shard_map/dot_general | solution.py:49
  479.0 9.2 %fusion = bf16[512,8192]{0,1:T(8,128)(2,1)} fusion(f32[8192,512]{1,0:T(8,128)} %fusion.3, bf16[512,64]{0,1:T(8,128)(2,1)S(1)} %convolution_convert_fusion.1, bf16[64,8192]{1,0:T(8,128)(2,1)S(1)} %copy-done.5), kind=kOutput, calls=%fused_computation.1 | convolution fusion | flops 549453824 | bytes 26279936 | tf_op jit(solution)/shard_map/dot_general | solution.py:55
  488.3 11.9 %copy.15 = bf16[512,8192]{1,0:T(8,128)(2,1)} copy(bf16[512,8192]{0,1:T(8,128)(2,1)} %fusion) | data formatting | bytes 16777216
  (28 shorter events, 1.6 us)
Async XLA Ops:
  7.2 16.1 %copy-start = (bf16[512,1024]{1,0:T(8,128)(2,1)S(1)}, bf16[512,1024]{1,0:T(8,128)(2,1)}, u32[]{:S(2)}) copy-start(bf16[512,1024]{1,0:T(8,128)(2,1)} %param.8) | copy-start | bytes 3145732
  7.2 33.2 %all-gather.5.cloned.1.call-start = ((), (), s32[]{:S(2)}) async-start(), calls=%async_computation.3 | async-start | bytes 1310720 | tf_op jit(solution)/shard_map/all_gather | solution.py:41
  7.9 112.2 %reduce-scatter.5.cloned.1.call-start = ((), (), s32[]{:S(2)}) async-start(), calls=%async_computation.5 | async-start | bytes 327680 | tf_op jit(solution)/shard_map/reduce_scatter | solution.py:64
  47.5 72.6 %reduce-scatter.3.cloned.1.call-start = ((), (), s32[]{:S(2)}) async-start(), calls=%async_computation.4 | async-start | bytes 2621440 | tf_op jit(solution)/shard_map/reduce_scatter | solution.py:63
  53.9 121.2 %all-reduce.3.cloned.1.call-start = ((), (), s32[]{:S(2)}) async-start(), calls=%async_computation.6 | async-start | bytes 1179648 | tf_op jit(solution)/shard_map/psum | solution.py:65
  56.6 1.4 copy-start.1
  56.6 2.0 copy-start.2
  56.6 2.7 copy-start.3
  92.7 11.8 %copy-start.7 = (f32[1024]{0:T(1024)S(1)}, f32[1024]{0:T(1024)}, u32[]{:S(2)}) copy-start(f32[1024]{0:T(1024)} %param.11) | copy-start | bytes 12292
  92.7 11.8 %copy-start.6 = (s32[32,1024]{1,0:T(8,128)S(1)}, s32[32,1024]{1,0:T(8,128)}, u32[]{:S(2)}) copy-start(s32[32,1024]{1,0:T(8,128)} %param.10) | copy-start | bytes 393220
  110.0 10.2 %copy-start.4 = (pred[2048,1024]{1,0:T(8,128)(4,1)S(1)}, pred[2048,1024]{1,0:T(8,128)(4,1)}, u32[]{:S(2)}) copy-start(pred[2048,1024]{1,0:T(8,128)(4,1)} %eq.156) | copy-start | bytes 6291460
  120.2 343.1 %all-gather.3.cloned.1.call-start = ((), (), s32[]{:S(2)}) async-start(), calls=%async_computation.2 | async-start | bytes 20971520 | tf_op jit(solution)/shard_map/all_gather | solution.py:51
  178.5 300.5 %copy-start.5 = (bf16[64,8192]{1,0:T(8,128)(2,1)S(1)}, bf16[64,8192]{1,0:T(8,128)(2,1)}, u32[]{:S(2)}) copy-start(bf16[64,8192]{1,0:T(8,128)(2,1)} %all-gather.5.cloned.1.call-done) | copy-start | bytes 3145732
Sparse Core Ops, SparseCore 0:
  9.6 30.7 all-gather.4
  47.7 19.5 reduce-scatter.4
  69.6 41.8 reduce-scatter.2
  120.3 54.8 all-reduce.2
  177.1 286.0 all-gather.2
where the time goes:
time: 508 us; the launch traced here: 507 us
  waiting for transfers between devices  347 us (68%)
  local copies, waits for them, and re-layouts  62.1 us (12%)
  matrix products  38.9 us (8%)
  other arithmetic  29.5 us (6%)
  blocking collectives  15.3 us (3%)
  between operations  13.9 us (3%)
    all_gather x1, waiting for transfers between devices, local(): lax.all_gather(local_rows, 'fsdp', axis=0, tiled=True)  285 us
    psum x1, waiting for transfers between devices, local(): summed_down, summed_up = lax.psum((shard_down, shard_up), 'dp')  44.5 us
    select_n x2, local copies, waits for them, and re-layouts, dequantize(): levels = jnp.where(nibbles == position, jnp.float32(quantum), levels)  23.9 us
    all_gather x1, waiting for transfers between devices, local(): lax.all_gather(down_adapter, 'fsdp', axis=1, tiled=True)  16.7 us
    dot_general x1, matrix products, local(): lax.dot_general(grad_out, lax.all_gather(local_rows, 'fsdp', axis=0, tile...  15.8 us
    mul x2, local copies, waits for them, and re-layouts, dequantize(): weight = levels * absmax[:, None, None, :]  15.7 us
    all_gather x1, blocking collectives, local(): lax.all_gather(up_adapter, 'fsdp', axis=1, tiled=True)  15.3 us
    unnamed x17, local copies, waits for them, and re-layouts  14.6 us
  transfers between devices with their start and end apart: 5, of which 3 were waited for; matrix products, arithmetic and copies ran while one was open for 17% of the time, Pallas kernels for 0%

commit v1 on v0

v1 whole, which is shorter than its diff:
```python
import functools

import jax
import jax.numpy as jnp
from jax import lax
from jax.experimental import pallas as pl
from jax.experimental.pallas import tpu as pltpu
from jax.sharding import PartitionSpec as P

MESH = pl.DeviceIdType.MESH
NT = (((1,), (1,)), ((), ()))
adapter_scale = 0.5
nf4_table = [
    -1.0,
    -0.6961928009986877,
    -0.5250730514526367,
    -0.39491748809814453,
    -0.28444138169288635,
    -0.18477343022823334,
    -0.09105003625154495,
    0.0,
    0.07958029955625534,
    0.16093020141124725,
    0.24611230194568634,
    0.33791524171829224,
    0.44070982933044434,
    0.5626170039176941,
    0.7229568362236023,
    1.0,
]
GROUP = 8


def levels_of(words, nibble):
    rows = [jnp.float32(v) for v in nf4_table]
    for bit in range(4):
        on = (words & (1 << (4 * nibble + bit))) != 0
        rows = [jnp.where(on, rows[2 * i + 1], rows[2 * i]) for i in range(len(rows) // 2)]
    return rows[0]


def kernel(Z, DP, factor, acts_hbm, grad_hbm, codes_hbm, scale_ref, col_ref, down_hbm, up_hbm,
           out_hbm, gdown_ref, gup_ref,
           acts, grad, codes, weight, downf, upf, stage, outb, mix, terms,
           g1s, g1r, g2s, g2r, g3r, fin,
           load_sem, down_sem, out_sem, send_sem, w_sem, d_sem, u_sem, g1_sem, g2_sem, g3_sem, g4_sem):
    d, z = lax.axis_index("dp"), lax.axis_index("fsdp")
    p, core = lax.rem(d, GROUP), lax.rem(d, 2)
    xbit, ybit = lax.rem(d // 2, 2), lax.rem(d // 4, 2)
    dx, dy, ds_ = 2 - 4 * xbit, 4 - 8 * ybit, 1 - 2 * core
    half_rows, width = weight.shape[3], weight.shape[4]
    tile = 2 * half_rows
    shard = GROUP * tile
    R = mix.shape[1]
    RH = R // 2
    up_width = upf.shape[2]
    half_blocks = half_rows // 64

    def source(k):
        m = jnp.minimum(z, Z - 1 - z)
        paired = jnp.where(k % 2 == 0, z - (k // 2 + 1), z + (k // 2 + 1))
        rest = jnp.where(2 * z < Z - 1, z + (k - m + 1), z - (k - m + 1))
        return jnp.where(k < 2 * m, paired, rest)

    at_x, at_y, at_s, at_d = (d + dx, z), (d + dy, z), (d + ds_, z), (d + dx + dy, z)
    pairs = DP // 2
    others = [lax.rem(d + 2 * j, DP) for j in range(1, pairs)]

    loads = [
        pltpu.make_async_copy(codes_hbm, codes, load_sem.at[0]),
        pltpu.make_async_copy(up_hbm, upf.at[z], load_sem.at[1]),
        pltpu.make_async_copy(grad_hbm, grad, load_sem.at[2]),
        pltpu.make_async_copy(acts_hbm, acts, load_sem.at[3]),
    ]
    down_loads = [
        pltpu.make_async_copy(down_hbm.at[:, q * tile:(q + 1) * tile], downf.at[z, q], down_sem.at[q])
        for q in range(GROUP)
    ]
    loads[0].start()
    loads[1].start()
    for c in down_loads:
        c.start()
    loads[2].start()
    loads[3].start()

    barrier = pltpu.get_barrier_semaphore()
    for k in range(Z - 1):
        pl.semaphore_signal(barrier, inc=1, device_id=(d, source(k)), device_id_type=MESH)
    for o in others:
        pl.semaphore_signal(barrier, inc=1, device_id=(o, z), device_id_type=MESH)
    pl.semaphore_signal(barrier, inc=1, device_id=at_s, device_id_type=MESH)

    sends = []

    def send(src, dst, sem, to):
        c = pltpu.make_async_remote_copy(src_ref=src, dst_ref=dst, send_sem=send_sem.at[len(sends)],
                                         recv_sem=sem, device_id=to, device_id_type=MESH)
        c.start()
        sends.append(c)

    def arrived(ref, sem):
        pltpu.make_async_remote_copy(src_ref=ref, dst_ref=ref, send_sem=send_sem.at[0], recv_sem=sem,
                                     device_id=at_s, device_id_type=MESH).wait_recv()

    def send_w(s, h, q, to):
        send(weight.at[s, h, q], weight.at[s, h, q], w_sem.at[s, h, q], to)

    def wait_w(s, h, q):
        arrived(weight.at[s, h, q], w_sem.at[s, h, q])

    def send_d(s, q, to):
        send(downf.at[s, q], downf.at[s, q], d_sem.at[s, q], to)

    def wait_d(s, q):
        arrived(downf.at[s, q], d_sem.at[s, q])

    def dequantize(h, q):
        for r in range(half_blocks):
            b = (h * GROUP + q) * half_blocks + r

            def columns(c, _, b=b, r=r):
                cols = pl.ds(pl.multiple_of(c * 256, 256), 256)
                words = codes[b, :, cols]
                absmax = (scale_ref[pl.ds(b, 1), cols].astype(jnp.float32) + 1.0) / 256.0 * col_ref[:, cols]
                for j in range(4):
                    stage[pl.ds(j, 16, stride=4), :] = levels_of(words, j)[:, :128] * absmax[:, :128]
                    stage[pl.ds(64 + j, 16, stride=4), :] = levels_of(words, j)[:, 128:] * absmax[:, 128:]
                weight[z, h, q, pl.ds(r * 64, 64), pl.ds(pl.multiple_of(c * 256, 128), 128)] = stage[0:64].astype(jnp.bfloat16)
                weight[z, h, q, pl.ds(r * 64, 64), pl.ds(pl.multiple_of(c * 256 + 128, 128), 128)] = stage[64:128].astype(jnp.bfloat16)
                return 0

            lax.fori_loop(0, width // 256, columns, 0)

    def tiles(s, h):
        def one(t, _):
            rows = weight[s, h, pl.ds(2 * t, 2)].reshape(tile, width)
            tt = h * 4 + t
            acc = lax.dot_general(grad[...], rows, NT, preferred_element_type=jnp.float32)
            acc += adapter_scale * jnp.dot(mix[...], downf[s, tt], preferred_element_type=jnp.float32)
            slot = s * GROUP + tt
            outb[slot] = acc.astype(jnp.bfloat16)
            pltpu.make_async_copy(outb.at[slot], out_hbm.at[:, pl.ds(pl.multiple_of(slot * tile, tile), tile)],
                                  out_sem.at[slot]).start()
            return 0

        lax.fori_loop(0, 4, one, 0)

    px, py, ps = p + dx, p + dy, p + ds_
    pd = p + dx + dy
    same_core = (p, px, py, pd)
    events = 2 * (Z - 1)

    def service(i):
        if 0 <= i < events:
            s, h = source(i // 2), i % 2
            wait_w(s, h, p)
            send_w(s, h, p, at_x)
            send_w(s, h, p, at_y)
            send_w(s, h, p, at_s)
        if 0 <= i - 1 < events:
            s, h = source((i - 1) // 2), (i - 1) % 2
            wait_w(s, h, px)
            if h == 0:
                send_w(s, h, px, at_y)
            send_w(s, h, px, at_s)
            wait_w(s, h, py)
            if h == 1:
                send_w(s, h, py, at_x)
            send_w(s, h, py, at_s)
        if 0 <= i - 2 < events:
            s, h = source((i - 2) // 2), (i - 2) % 2
            wait_w(s, h, pd)
            send_w(s, h, pd, at_s)
        if 0 <= i - 3 < events:
            s, h = source((i - 3) // 2), (i - 3) % 2
            for q in same_core:
                wait_w(s, h, q + ds_)
            tiles(s, h)

    def own(h):
        def one(j, _):
            dequantize(h, lax.rem(p + j, GROUP))
            return 0

        lax.fori_loop(1, GROUP, one, 0)
        tiles(z, h)

    loads[0].wait()
    dequantize(0, p)
    pl.semaphore_wait(barrier, (Z - 1) + (pairs - 1) + 1)
    loads[1].wait()
    for k in range(Z - 1):
        send(upf.at[z], upf.at[z], u_sem.at[z], (d, source(k)))
    for c in down_loads:
        c.wait()
    for k in range(Z - 1):
        send_d(z, p, (d, source(k)))
    for k in range(Z - 1):
        if k == 0:
            send_w(z, 0, p, (d, source(k)))
            dequantize(1, p)
        else:
            send_w(z, 0, p, (d, source(k)))
        send_w(z, 1, p, (d, source(k)))

    loads[2].wait()
    for k in range(Z - 1):
        arrived(upf.at[source(k)], u_sem.at[source(k)])
    mixed = jnp.zeros(mix.shape, jnp.float32)
    for s in range(Z):
        mixed += lax.dot_general(grad[:, s * up_width:(s + 1) * up_width], upf[s], NT,
                                 preferred_element_type=jnp.float32)
    mix[...] = mixed.astype(jnp.bfloat16)

    def down_first():
        for k in range(Z - 1):
            s = source(k)
            wait_d(s, p)
            for to in (at_x, at_y, at_d, at_s):
                send_d(s, p, to)

    def down_second():
        for k in range(Z - 1):
            s = source(k)
            for q in (px, py, pd):
                wait_d(s, q)
                send_d(s, q, at_s)

    def down_third():
        for k in range(Z - 1):
            for q in same_core:
                wait_d(source(k), q + ds_)

    def gradient_terms():
        loads[3].wait()
        mixed_t = mix[...].astype(jnp.float32).T.astype(jnp.bfloat16)

        def one(t, low):
            s, q = t // GROUP, lax.rem(t, GROUP)
            a = acts[:, pl.ds(pl.multiple_of(t * tile, tile), tile)]
            terms[s, :, pl.ds(pl.multiple_of(q * tile, tile), tile)] = jnp.dot(
                mixed_t, a, preferred_element_type=jnp.float32)
            return low + lax.dot_general(a, downf[s, q], NT, preferred_element_type=jnp.float32)

        low = lax.fori_loop(0, Z * GROUP, one, jnp.zeros(mix.shape, jnp.float32))
        low_t = low.astype(jnp.bfloat16).astype(jnp.float32).T.astype(jnp.bfloat16)
        for s in range(Z):
            terms[s, :, shard:shard + up_width] = jnp.dot(
                low_t, grad[:, s * up_width:(s + 1) * up_width], preferred_element_type=jnp.float32)
        mine, theirs = pl.multiple_of(core * RH, RH), pl.multiple_of((1 - core) * RH, RH)
        for s in range(Z):
            g1s[s] = terms[s, pl.ds(theirs, RH), :].astype(jnp.bfloat16)
        send(g1s, g1r, g1_sem.at[0], at_s)

    def reduce_core():
        arrived(g1r, g1_sem.at[0])
        mine = pl.multiple_of(core * RH, RH)
        for s in range(Z):
            total = terms[s, pl.ds(mine, RH), :] + g1r[s].astype(jnp.float32)
            terms[s, pl.ds(mine, RH), :] = total
            g2s[s] = total.astype(jnp.bfloat16)
        for k in range(Z - 1):
            s = source(k)
            send(g2s.at[s], g2r.at[z], g2_sem.at[z], (d, s))

    def reduce_fsdp():
        mine = pl.multiple_of(core * RH, RH)
        total = terms[z, pl.ds(mine, RH), :]
        for k in range(Z - 1):
            s = source(k)
            arrived(g2r.at[s], g2_sem.at[s])
            total += g2r[s].astype(jnp.float32)
        slot = d // 2
        g3r[slot] = total.astype(jnp.bfloat16)
        for o in others:
            send(g3r.at[slot], g3r.at[slot], g3_sem.at[slot], (o, z))

    def reduce_dp():
        for o in others:
            arrived(g3r.at[o // 2], g3_sem.at[o // 2])
        total = g3r[0].astype(jnp.float32)
        for j in range(1, pairs):
            total += g3r[j].astype(jnp.float32)
        fin[core] = factor * total
        send(fin.at[core], fin.at[core], g4_sem.at[0], at_s)

    def finish():
        arrived(fin.at[1 - core], g4_sem.at[0])
        for c in range(2):
            gdown_ref[c * RH:(c + 1) * RH, :] = fin[c, :, :shard]
            gup_ref[c * RH:(c + 1) * RH, :] = fin[c, :, shard:shard + up_width]

    work = [
        lambda: (down_first(), own(0)),
        lambda: (down_second(), own(1)),
        lambda: (down_third(), gradient_terms()),
        reduce_core,
        reduce_fsdp,
        reduce_dp,
        finish,
    ]
    for i in range(events + 3):
        service(i)
        if i < len(work):
            work[i]()
    for c in sends:
        c.wait_send()

    def drain(t, _):
        pltpu.make_async_copy(outb.at[t], out_hbm.at[:, pl.ds(pl.multiple_of(t * tile, tile), tile)],
                              out_sem.at[t]).wait()
        return 0

    lax.fori_loop(0, Z * GROUP, drain, 0)


def solution(mesh):
    Z, DP = mesh.shape["fsdp"], mesh.shape["dp"]
    bf16, f32 = jnp.bfloat16, jnp.float32

    def local(acts, grad_out, codes, scale_codes, col_scale, down_adapter, up_adapter):
        tokens, D = acts.shape
        O = grad_out.shape[1]
        R, shard = down_adapter.shape
        up_width = up_adapter.shape[1]
        tile = shard // GROUP
        wide = shard + up_width
        RH = R // 2
        factor = adapter_scale * float(tokens * Z * DP) ** (-0.5)
        n_sends = (Z - 1) * (1 + 1 + 2 + 2 * 8 + 4 + 3 + 1) + 1 + (DP // 2 - 1) + 1
        DMA = pltpu.SemaphoreType.DMA
        anywhere, vmem = pl.BlockSpec(memory_space=pl.ANY), pl.BlockSpec(memory_space=pltpu.VMEM)
        return pl.pallas_call(
            functools.partial(kernel, Z, DP, factor),
            out_shape=(
                jax.ShapeDtypeStruct((tokens, D), bf16),
                jax.ShapeDtypeStruct((R, shard), f32),
                jax.ShapeDtypeStruct((R, up_width), f32),
            ),
            in_specs=[anywhere, anywhere, anywhere, vmem, vmem, anywhere, anywhere],
            out_specs=(anywhere, vmem, vmem),
            scratch_shapes=[
                pltpu.VMEM((tokens, D), bf16),
                pltpu.VMEM((tokens, O), bf16),
                pltpu.VMEM(codes.shape, jnp.int32),
                pltpu.VMEM((Z, 2, GROUP, tile // 2, O), bf16),
                pltpu.VMEM((Z, GROUP, R, tile), bf16),
                pltpu.VMEM((Z, R, up_width), bf16),
                pltpu.VMEM((128, 128), f32),
                pltpu.VMEM((Z * GROUP, tokens, tile), bf16),
                pltpu.VMEM((tokens, R), bf16),
                pltpu.VMEM((Z, R, wide), f32),
                pltpu.VMEM((Z, RH, wide), bf16),
                pltpu.VMEM((Z, RH, wide), bf16),
                pltpu.VMEM((Z, RH, wide), bf16),
                pltpu.VMEM((Z, RH, wide), bf16),
                pltpu.VMEM((DP // 2, RH, wide), bf16),
                pltpu.VMEM((2, RH, wide), f32),
                DMA((4,)), DMA((GROUP,)), DMA((Z * GROUP,)), DMA((n_sends,)),
                DMA((Z, 2, GROUP)), DMA((Z, GROUP)), DMA((Z,)),
                DMA((1,)), DMA((Z,)), DMA((DP // 2,)), DMA((1,)),
            ],
            compiler_params=pltpu.CompilerParams(
                collective_id=0, has_side_effects=True, vmem_limit_bytes=60 * 1024 * 1024
            ),
        )(acts, grad_out, codes, scale_codes, col_scale.reshape(1, -1), down_adapter, up_adapter)

    placed = (
        P(("dp", "fsdp"), None),
        P(("dp", "fsdp"), None),
        P("fsdp", None, None),
        P("fsdp", None),
        P(),
        P(None, "fsdp"),
        P(None, "fsdp"),
    )
    return jax.shard_map(
        local,
        mesh=mesh,
        in_specs=placed,
        out_specs=(P(("dp", "fsdp"), None), P(None, "fsdp"), P(None, "fsdp")),
        check_vma=False,
    )
```

time: 508 us -> 121 us (0.24)
  waiting for transfers between devices: 347 us -> 0 us
  Pallas kernels: 0 us -> 111 us
  local copies, waits for them, and re-layouts: 62.1 us -> 9.26 us
  matrix products: 38.9 us -> 0 us
  other arithmetic: 29.5 us -> 0 us
  blocking collectives: 15.3 us -> 0 us
  between operations: 13.9 us -> 0.66 us
    all_gather x2 -> x0, waiting for transfers between devices: 301 us -> none  [the longest x1 285 us: local(): lax.all_gather(local_rows, 'fsdp', axis=0, tiled=True)]
    pallas_call x0 -> x1, Pallas kernels: none -> 111 us  [local(): pl.pallas_call(functools.partial(kernel, Z, DP, factor), out_shape=(jax.S...]
    psum x1 -> x0, waiting for transfers between devices: 44.5 us -> none  [local(): summed_down, summed_up = lax.psum((shard_down, shard_up), 'dp')]
    dot_general x5 -> x0, matrix products: 38.9 us -> none  [the longest x1 15.8 us: local(): lax.dot_general(grad_out, lax.all_gather(local_rows, 'fsdp', axis=0, tile...]
    select_n x2 -> x0, local copies, waits for them, and re-layouts: 23.9 us -> none  [dequantize(): levels = jnp.where(nibbles == position, jnp.float32(quantum), levels)]
    mul x2 -> x0, local copies, waits for them, and re-layouts: 15.7 us -> none  [dequantize(): weight = levels * absmax[:, None, None, :]]
    all_gather x1 -> x0, blocking collectives: 15.3 us -> none  [local(): lax.all_gather(up_adapter, 'fsdp', axis=1, tiled=True)]
    convert_element_type x1 -> x0, other arithmetic: 10.4 us -> none  [dequantize(): return weight.reshape(block_count * 64, columns).astype(jnp.bfloat16)]
  transfers between devices with their start and end apart: 5 -> 0, of which waited for: 3 -> 0; matrix products, arithmetic and copies ran while one was open for 17% -> 0% of each run, Pallas kernels for 0% -> 0%
where the time goes in v1:
time: 121 us
  Pallas kernels  111 us (92%)
  local copies, waits for them, and re-layouts  9.26 us (8%)
    pallas_call x1, Pallas kernels, local(): pl.pallas_call(functools.partial(kernel, Z, DP, factor), out_shape=(jax.S...  111 us
    unnamed x7, local copies, waits for them, and re-layouts  9.26 us

profile of v1, /device:TPU:0, one launch (start us, length us, event | category | flops | bytes accessed | tf_op | source)
XLA Modules:
  0.0 120.7 jit_solution(417563427676545776)
XLA Ops:
  0.6 110.8 %shard_map.94 = (bf16[512,8192]{1,0:T(8,128)(2,1)}, f32[64,2048]{1,0:T(8,128)}, f32[64,256]{1,0:T(8,128)}) custom-call(bf16[512,8192]{1,0:T(8,128)(2,1)} %acts_hbm.1, bf16[512,1024]{1,0:T(8,128)(2,1)} %grad_hbm.1, s32[32,16,1024]{2,1,0:T(8,128)} %codes_hbm.1, s32[32,1024]{1,0:T(8,128)} %scale_ref.1, f32[1,1024]{1,0:T(1,128)} %bitcast.1, ...), custom_call_target="tpu_custom_call" | custom-call | tf_op jit(solution)/shard_map/pallas_call | solution.py:333
  111.4 0.0 copy-start
  111.4 0.0 copy-start.1
  111.4 7.8 %copy.13 = bf16[512,8192]{1,0:T(8,128)(2,1)} copy(bf16[512,8192]{1,0:T(8,128)(2,1)} %get-tuple-element.6) | data formatting | bytes 16777216
  119.3 0.0 copy-done
  119.3 0.8 copy.14
  120.1 0.0 copy-done.1
  120.1 0.6 copy.15
Async XLA Ops:
  111.4 7.9 %copy-start = (f32[64,2048]{1,0:T(8,128)S(1)}, f32[64,2048]{1,0:T(8,128)}, u32[]{:S(2)}) copy-start(f32[64,2048]{1,0:T(8,128)} %get-tuple-element.7) | copy-start | bytes 1572868
  111.4 8.6 %copy-start.1 = (f32[64,256]{1,0:T(8,128)S(1)}, f32[64,256]{1,0:T(8,128)}, u32[]{:S(2)}) copy-start(f32[64,256]{1,0:T(8,128)} %get-tuple-element.8) | copy-start | bytes 196612

commit v2 on v1

--- a/solution.py
+++ b/solution.py
@@ -90,13 +90,20 @@
         pl.semaphore_signal(barrier, inc=1, device_id=(o, z), device_id_type=MESH)
     pl.semaphore_signal(barrier, inc=1, device_id=at_s, device_id_type=MESH)
 
-    sends = []
+    sends, conditions = [], {}
 
     def send(src, dst, sem, to):
         c = pltpu.make_async_remote_copy(src_ref=src, dst_ref=dst, send_sem=send_sem.at[len(sends)],
                                          recv_sem=sem, device_id=to, device_id_type=MESH)
         c.start()
         sends.append(c)
+
+    def send_if(on, src, dst, sem, to):
+        c = pltpu.make_async_remote_copy(src_ref=src, dst_ref=dst, send_sem=send_sem.at[len(sends)],
+                                         recv_sem=sem, device_id=to, device_id_type=MESH)
+        pl.when(on)(c.start)
+        sends.append(c)
+        conditions[len(sends) - 1] = on
 
     def arrived(ref, sem):
         pltpu.make_async_remote_copy(src_ref=ref, dst_ref=ref, send_sem=send_sem.at[0], recv_sem=sem,
@@ -150,13 +157,28 @@
     same_core = (p, px, py, pd)
     events = 2 * (Z - 1)
 
-    def service(i):
+    def passes_on(s):
+        return ((s < z) & (z < Z - 1)) | ((s > z) & (z > 0))
+
+    def pass_on(i):
         if 0 <= i < events:
             s, h = source(i // 2), i % 2
-            wait_w(s, h, p)
+            on = passes_on(s)
+            pl.when(on)(lambda: wait_w(s, h, p))
+            piece = weight.at[s, h, p]
+            to = jnp.where(on, z + jnp.where(s < z, 1, -1), source(0))
+            send_if(on, piece, piece, w_sem.at[s, h, p], (d, to))
+
+    def service(i):
+        if i < 2:
+            pass_on(i)
+        if 0 <= i < events:
+            s, h = source(i // 2), i % 2
+            pl.when(jnp.logical_not(passes_on(s)))(lambda: wait_w(s, h, p))
             send_w(s, h, p, at_x)
             send_w(s, h, p, at_y)
             send_w(s, h, p, at_s)
+        pass_on(i + 2)
         if 0 <= i - 1 < events:
             s, h = source((i - 1) // 2), (i - 1) % 2
             wait_w(s, h, px)
@@ -195,13 +217,12 @@
         c.wait()
     for k in range(Z - 1):
         send_d(z, p, (d, source(k)))
-    for k in range(Z - 1):
-        if k == 0:
-            send_w(z, 0, p, (d, source(k)))
+    for h in range(2):
+        piece = weight.at[z, h, p]
+        for on, to in ((z < Z - 1, jnp.where(z < Z - 1, z + 1, z - 1)), (z > 0, jnp.where(z > 0, z - 1, z + 1))):
+            send_if(on, piece, piece, w_sem.at[z, h, p], (d, to))
+        if h == 0:
             dequantize(1, p)
-        else:
-            send_w(z, 0, p, (d, source(k)))
-        send_w(z, 1, p, (d, source(k)))
 
     loads[2].wait()
     for k in range(Z - 1):
@@ -303,8 +324,11 @@
         service(i)
         if i < len(work):
             work[i]()
-    for c in sends:
-        c.wait_send()
+    for j, c in enumerate(sends):
+        if j in conditions:
+            pl.when(conditions[j])(c.wait_send)
+        else:
+            c.wait_send()
 
     def drain(t, _):
         pltpu.make_async_copy(outb.at[t], out_hbm.at[:, pl.ds(pl.multiple_of(t * tile, tile), tile)],
@@ -327,7 +351,7 @@
         wide = shard + up_width
         RH = R // 2
         factor = adapter_scale * float(tokens * Z * DP) ** (-0.5)
-        n_sends = (Z - 1) * (1 + 1 + 2 + 2 * 8 + 4 + 3 + 1) + 1 + (DP // 2 - 1) + 1
+        n_sends = 4 + (Z - 1) * (1 + 1 + 2 * 9 + 4 + 3 + 1) + 1 + (DP // 2 - 1) + 1
         DMA = pltpu.SemaphoreType.DMA
         anywhere, vmem = pl.BlockSpec(memory_space=pl.ANY), pl.BlockSpec(memory_space=pltpu.VMEM)
         return pl.pallas_call(

time: 121 us -> 107 us (0.88)
  Pallas kernels: 111 us -> 97.2 us
    pallas_call x1, Pallas kernels: 111 us -> 97.2 us  [local(): pl.pallas_call(functools.partial(kernel, Z, DP, factor), out_shape=(jax.S...]
where the time goes in v2:
time: 107 us
  Pallas kernels  97.2 us (91%)
  local copies, waits for them, and re-layouts  9.26 us (9%)
    pallas_call x1, Pallas kernels, local(): pl.pallas_call(functools.partial(kernel, Z, DP, factor), out_shape=(jax.S...  97.2 us
    unnamed x7, local copies, waits for them, and re-layouts  9.26 us

profile of v2, /device:TPU:0, one launch (start us, length us, event | category | flops | bytes accessed | tf_op | source)
XLA Modules:
  0.0 107.1 jit_solution(8745927487219940938)
XLA Ops:
  0.6 97.2 %shard_map.94 = (bf16[512,8192]{1,0:T(8,128)(2,1)}, f32[64,2048]{1,0:T(8,128)}, f32[64,256]{1,0:T(8,128)}) custom-call(bf16[512,8192]{1,0:T(8,128)(2,1)} %acts_hbm.1, bf16[512,1024]{1,0:T(8,128)(2,1)} %grad_hbm.1, s32[32,16,1024]{2,1,0:T(8,128)} %codes_hbm.1, s32[32,1024]{1,0:T(8,128)} %scale_ref.1, f32[1,1024]{1,0:T(1,128)} %bitcast.1, ...), custom_call_target="tpu_custom_call" | custom-call | tf_op jit(solution)/shard_map/pallas_call | solution.py:357
  97.9 0.0 copy-start
  97.9 0.0 copy-start.1
  97.9 7.8 %copy.13 = bf16[512,8192]{1,0:T(8,128)(2,1)} copy(bf16[512,8192]{1,0:T(8,128)(2,1)} %get-tuple-element.6) | data formatting | bytes 16777216
  105.7 0.0 copy-done
  105.7 0.8 copy.14
  106.5 0.0 copy-done.1
  106.5 0.6 copy.15
Async XLA Ops:
  97.9 7.9 %copy-start = (f32[64,2048]{1,0:T(8,128)S(1)}, f32[64,2048]{1,0:T(8,128)}, u32[]{:S(2)}) copy-start(f32[64,2048]{1,0:T(8,128)} %get-tuple-element.7) | copy-start | bytes 1572868
  97.9 8.6 %copy-start.1 = (f32[64,256]{1,0:T(8,128)S(1)}, f32[64,256]{1,0:T(8,128)}, u32[]{:S(2)}) copy-start(f32[64,256]{1,0:T(8,128)} %get-tuple-element.8) | copy-start | bytes 196612

commit v3 on v2

--- a/solution.py
+++ b/solution.py
@@ -169,42 +169,73 @@
             to = jnp.where(on, z + jnp.where(s < z, 1, -1), source(0))
             send_if(on, piece, piece, w_sem.at[s, h, p], (d, to))
 
+    def at_end(s):
+        return (s == 0) | (s == Z - 1)
+
+    def pass_on_diagonal(i):
+        for s in (0, Z - 1):
+            away = z if s == 0 else Z - 1 - z
+            for h in range(2):
+                if not 1 <= i - 1 - h <= Z - 2:
+                    continue
+                on = away == i - 1 - h
+                piece = weight.at[s, h, pd]
+                pl.when(on)(lambda s=s, h=h: wait_w(s, h, pd))
+                to = jnp.where(on, z + (1 if s == 0 else -1), source(0))
+                send_if(on, piece, piece, w_sem.at[s, h, pd], (d, to))
+
+    def event(i):
+        return source(i // 2), i % 2
+
+    def first(i):
+        s, h = event(i)
+        pl.when(jnp.logical_not(passes_on(s)))(lambda: wait_w(s, h, p))
+        send_w(s, h, p, at_x)
+        send_w(s, h, p, at_y)
+        send_w(s, h, p, at_s)
+
+    def second(i):
+        s, h = event(i)
+        inner = jnp.logical_not(at_end(s))
+        wait_w(s, h, px)
+        if h == 0:
+            piece = weight.at[s, h, px]
+            send_if(inner, piece, piece, w_sem.at[s, h, px], at_y)
+        send_w(s, h, px, at_s)
+        wait_w(s, h, py)
+        if h == 1:
+            piece = weight.at[s, h, py]
+            send_if(inner, piece, piece, w_sem.at[s, h, py], at_x)
+        send_w(s, h, py, at_s)
+
+    def third(i):
+        s, h = event(i)
+        pl.when(jnp.logical_not(at_end(s) & passes_on(s)))(lambda: wait_w(s, h, pd))
+        send_w(s, h, pd, at_s)
+
+    def use(i):
+        s, h = event(i)
+        for q in same_core:
+            wait_w(s, h, q + ds_)
+        tiles(s, h)
+
     def service(i):
         if i < 2:
             pass_on(i)
-        if 0 <= i < events:
-            s, h = source(i // 2), i % 2
-            pl.when(jnp.logical_not(passes_on(s)))(lambda: wait_w(s, h, p))
-            send_w(s, h, p, at_x)
-            send_w(s, h, p, at_y)
-            send_w(s, h, p, at_s)
+        first(i)
         pass_on(i + 2)
-        if 0 <= i - 1 < events:
-            s, h = source((i - 1) // 2), (i - 1) % 2
-            wait_w(s, h, px)
-            if h == 0:
-                send_w(s, h, px, at_y)
-            send_w(s, h, px, at_s)
-            wait_w(s, h, py)
-            if h == 1:
-                send_w(s, h, py, at_x)
-            send_w(s, h, py, at_s)
-        if 0 <= i - 2 < events:
-            s, h = source((i - 2) // 2), (i - 2) % 2
-            wait_w(s, h, pd)
-            send_w(s, h, pd, at_s)
-        if 0 <= i - 3 < events:
-            s, h = source((i - 3) // 2), (i - 3) % 2
-            for q in same_core:
-                wait_w(s, h, q + ds_)
-            tiles(s, h)
+        pass_on_diagonal(i)
+        for step, back in ((second, 1), (third, 2), (use, 3)):
+            if i >= back:
+                step(i - back)
 
     def own(h):
         def one(j, _):
-            dequantize(h, lax.rem(p + j, GROUP))
+            m = jnp.where(j == GROUP - 3, GROUP - 1, j + 1)
+            dequantize(h, p + lax.rem(m, 2) * ds_ + lax.rem(m // 2, 2) * dx + (m // 4) * dy)
             return 0
 
-        lax.fori_loop(1, GROUP, one, 0)
+        lax.fori_loop(0, GROUP - 2, one, 0)
         tiles(z, h)
 
     loads[0].wait()
@@ -223,6 +254,10 @@
             send_if(on, piece, piece, w_sem.at[z, h, p], (d, to))
         if h == 0:
             dequantize(1, p)
+    for h in range(2):
+        dequantize(h, pd)
+        piece = weight.at[z, h, pd]
+        send_if(at_end(z), piece, piece, w_sem.at[z, h, pd], (d, jnp.where(z == 0, z + 1, z - 1)))
 
     loads[2].wait()
     for k in range(Z - 1):
@@ -320,10 +355,18 @@
         reduce_dp,
         finish,
     ]
-    for i in range(events + 3):
+    for i in range(events):
         service(i)
         if i < len(work):
             work[i]()
+    use(events - 3)
+    third(events - 2)
+    use(events - 2)
+    for step in work[events:]:
+        step()
+    second(events - 1)
+    third(events - 1)
+    use(events - 1)
     for j, c in enumerate(sends):
         if j in conditions:
             pl.when(conditions[j])(c.wait_send)
@@ -351,7 +394,7 @@
         wide = shard + up_width
         RH = R // 2
         factor = adapter_scale * float(tokens * Z * DP) ** (-0.5)
-        n_sends = 4 + (Z - 1) * (1 + 1 + 2 * 9 + 4 + 3 + 1) + 1 + (DP // 2 - 1) + 1
+        n_sends = 6 + 4 * (Z - 2) + (Z - 1) * (1 + 1 + 2 * 9 + 4 + 3 + 1) + 1 + (DP // 2 - 1) + 1
         DMA = pltpu.SemaphoreType.DMA
         anywhere, vmem = pl.BlockSpec(memory_space=pl.ANY), pl.BlockSpec(memory_space=pltpu.VMEM)
         return pl.pallas_call(

time: 107 us -> 104 us (0.972)
  Pallas kernels: 97.2 us -> 93.9 us
    pallas_call x1, Pallas kernels: 97.2 us -> 93.9 us  [local(): pl.pallas_call(functools.partial(kernel, Z, DP, factor), out_shape=(jax.S...]
where the time goes in v3:
time: 104 us
  Pallas kernels  93.9 us (90%)
  local copies, waits for them, and re-layouts  9.26 us (9%)
    pallas_call x1, Pallas kernels, local(): pl.pallas_call(functools.partial(kernel, Z, DP, factor), out_shape=(jax.S...  93.9 us
    unnamed x7, local copies, waits for them, and re-layouts  9.26 us

profile of v3, /device:TPU:0, one launch (start us, length us, event | category | flops | bytes accessed | tf_op | source)
XLA Modules:
  0.0 103.9 jit_solution(3209548895655451198)
XLA Ops:
  0.6 93.9 %shard_map.94 = (bf16[512,8192]{1,0:T(8,128)(2,1)}, f32[64,2048]{1,0:T(8,128)}, f32[64,256]{1,0:T(8,128)}) custom-call(bf16[512,8192]{1,0:T(8,128)(2,1)} %acts_hbm.1, bf16[512,1024]{1,0:T(8,128)(2,1)} %grad_hbm.1, s32[32,16,1024]{2,1,0:T(8,128)} %codes_hbm.1, s32[32,1024]{1,0:T(8,128)} %scale_ref.1, f32[1,1024]{1,0:T(1,128)} %bitcast.1, ...), custom_call_target="tpu_custom_call" | custom-call | tf_op jit(solution)/shard_map/pallas_call | solution.py:400
  94.6 0.0 copy-start
  94.6 0.0 copy-start.1
  94.6 7.8 %copy.13 = bf16[512,8192]{1,0:T(8,128)(2,1)} copy(bf16[512,8192]{1,0:T(8,128)(2,1)} %get-tuple-element.6) | data formatting | bytes 16777216
  102.4 0.0 copy-done
  102.4 0.8 copy.14
  103.2 0.0 copy-done.1
  103.2 0.6 copy.15
Async XLA Ops:
  94.6 7.9 %copy-start = (f32[64,2048]{1,0:T(8,128)S(1)}, f32[64,2048]{1,0:T(8,128)}, u32[]{:S(2)}) copy-start(f32[64,2048]{1,0:T(8,128)} %get-tuple-element.7) | copy-start | bytes 1572868
  94.6 8.6 %copy-start.1 = (f32[64,256]{1,0:T(8,128)S(1)}, f32[64,256]{1,0:T(8,128)}, u32[]{:S(2)}) copy-start(f32[64,256]{1,0:T(8,128)} %get-tuple-element.8) | copy-start | bytes 196612

commit v4 on v3

--- a/solution.py
+++ b/solution.py
@@ -347,9 +347,9 @@
             gup_ref[c * RH:(c + 1) * RH, :] = fin[c, :, shard:shard + up_width]
 
     work = [
-        lambda: (down_first(), own(0)),
-        lambda: (down_second(), own(1)),
+        lambda: (down_first(), down_second(), own(0)),
         lambda: (down_third(), gradient_terms()),
+        lambda: own(1),
         reduce_core,
         reduce_fsdp,
         reduce_dp,

time: 104 us -> 103 us (level)
  Pallas kernels: 93.9 us -> 92.5 us
    pallas_call x1, Pallas kernels: 93.9 us -> 92.5 us  [local(): pl.pallas_call(functools.partial(kernel, Z, DP, factor), out_shape=(jax.S...]
where the time goes in v4:
time: 103 us; the launch traced here: 102 us
  Pallas kernels  92.5 us (90%)
  local copies, waits for them, and re-layouts  9.26 us (9%)
    pallas_call x1, Pallas kernels, local(): pl.pallas_call(functools.partial(kernel, Z, DP, factor), out_shape=(jax.S...  92.5 us
    unnamed x7, local copies, waits for them, and re-layouts  9.26 us

profile of v4, /device:TPU:0, one launch (start us, length us, event | category | flops | bytes accessed | tf_op | source)
XLA Modules:
  0.0 102.4 jit_solution(14727112399681314177)
XLA Ops:
  0.6 92.5 %shard_map.94 = (bf16[512,8192]{1,0:T(8,128)(2,1)}, f32[64,2048]{1,0:T(8,128)}, f32[64,256]{1,0:T(8,128)}) custom-call(bf16[512,8192]{1,0:T(8,128)(2,1)} %acts_hbm.1, bf16[512,1024]{1,0:T(8,128)(2,1)} %grad_hbm.1, s32[32,16,1024]{2,1,0:T(8,128)} %codes_hbm.1, s32[32,1024]{1,0:T(8,128)} %scale_ref.1, f32[1,1024]{1,0:T(1,128)} %bitcast.1, ...), custom_call_target="tpu_custom_call" | custom-call | tf_op jit(solution)/shard_map/pallas_call | solution.py:400
  93.2 0.0 copy-start
  93.2 0.0 copy-start.1
  93.2 7.8 %copy.13 = bf16[512,8192]{1,0:T(8,128)(2,1)} copy(bf16[512,8192]{1,0:T(8,128)(2,1)} %get-tuple-element.6) | data formatting | bytes 16777216
  101.0 0.0 copy-done
  101.0 0.8 copy.14
  101.8 0.0 copy-done.1
  101.8 0.6 copy.15
Async XLA Ops:
  93.2 7.9 %copy-start = (f32[64,2048]{1,0:T(8,128)S(1)}, f32[64,2048]{1,0:T(8,128)}, u32[]{:S(2)}) copy-start(f32[64,2048]{1,0:T(8,128)} %get-tuple-element.7) | copy-start | bytes 1572868
  93.2 8.6 %copy-start.1 = (f32[64,256]{1,0:T(8,128)S(1)}, f32[64,256]{1,0:T(8,128)}, u32[]{:S(2)}) copy-start(f32[64,256]{1,0:T(8,128)} %get-tuple-element.8) | copy-start | bytes 196612
